TPU v7x, 32 devices: a whole 2x2x4 slice. The times are simulated.
32 devices in a mesh: col: 4 (over y, x), bulk: 8 (over z, core).
Axes of the slice: x: 2, y: 2, z: 4, core: 2. Of those that a mesh axis runs over, the one named last changes fastest.
Arguments:
- sequence_embedding: bfloat16 [64, 128, 64], P('bulk', 'col'), may hold values from -6 to 6
- residue_couplings: bfloat16 [128, 128, 128], P('bulk', 'col'), may hold values from -6 to 6
- sequence_layernorm_factor: float32 [64], replicated, may hold values from 0.5 to 1.5
- coupling_layernorm_factor: float32 [128], replicated, may hold values from 0.5 to 1.5
- content_projection: bfloat16 [64, 256], replicated, may hold values from -0.75 to 0.75
- switch_projection: bfloat16 [64, 256], replicated, may hold values from -0.75 to 0.75
- attention_score_projection: bfloat16 [128, 8], replicated, may hold values from -0.29882812 to 0.29882812
- final_projection: bfloat16 [256, 64], replicated, may hold values from -2 to 2
- residual_change_cotangent: bfloat16 [64, 128, 64], P('bulk', 'col'), may hold values from -6 to 6
Outputs:
- residual_change: bfloat16 [64, 128, 64], P('bulk', 'col')
- sequence_embedding_sensitivity: bfloat16 [64, 128, 64], P('bulk', 'col')
- coupling_sensitivity: bfloat16 [128, 128, 128], P('bulk', 'col')
All inputs are finite; a program needn't handle non-finite values.
Results may differ from a plain program's by a relative error of at most 0.025.
Values may be sent and summed in bfloat16 or wider, within the bound.
A program may use at most 64 MiB of HBM per device.

v0:
```python
import jax
import jax.numpy as jnp
from jax import lax
from jax.sharding import PartitionSpec as P

epsilon = 1e-05


def centred_sequences(inputs, scale_gain):
    widened = inputs.astype(jnp.float32)
    row_mean = jnp.mean(widened, axis=-1, keepdims=True)
    centered = widened - row_mean
    variance = jnp.mean(centered * centered, axis=-1, keepdims=True)
    inv_std = lax.rsqrt(variance + epsilon)
    normed = centered * inv_std
    return (normed * scale_gain, normed, inv_std)


def layernorm_reverse_mode(upstream, normed, inv_std, scale_gain):
    scaled = upstream * scale_gain
    mean_grad = jnp.mean(scaled, axis=-1, keepdims=True)
    mean_proj = jnp.mean(scaled * normed, axis=-1, keepdims=True)
    return inv_std * (scaled - mean_grad - normed * mean_proj)


def per_device(
    sequence_embedding,
    residue_couplings,
    sequence_layernorm_factor,
    coupling_layernorm_factor,
    content_projection,
    switch_projection,
    attention_score_projection,
    final_projection,
    residual_change_cotangent,
):
    number_of_heads = attention_score_projection.shape[1]
    value_channels = content_projection.shape[1]
    head_channels = value_channels // number_of_heads
    device_sequences = sequence_embedding.shape[0]
    device_residues = sequence_embedding.shape[1]
    finest_accuracy = lax.Precision.HIGHEST
    out_wide = final_projection.astype(jnp.float32)
    switch_single_form = switch_projection.astype(jnp.float32)
    bias_wide = attention_score_projection.astype(jnp.float32)
    pair_scaled, pair_hat, pair_inv = centred_sequences(
        residue_couplings, coupling_layernorm_factor
    )
    logits = jnp.einsum(
        "ijk,kh->hij",
        pair_scaled.astype(jnp.bfloat16),
        attention_score_projection,
        preferred_element_type=jnp.float32,
    )
    exponent = jnp.exp(logits)
    totals = lax.psum(jnp.sum(exponent, axis=2), "col")
    weights = exponent / totals[:, :, None]
    weights_low = weights.astype(jnp.bfloat16)
    weight_panel = lax.all_gather(weights_low, "bulk", axis=1, tiled=True)
    all_tokens = weight_panel.shape[1]
    sequence_scaled_by_factor, sequence_centred_unit, sequence_reciprocal_spread = (
        centred_sequences(sequence_embedding, sequence_layernorm_factor)
    )
    sequence_embedding_brief = sequence_scaled_by_factor.astype(jnp.bfloat16)
    content_sequences = jnp.dot(
        sequence_embedding_brief, content_projection, preferred_element_type=jnp.float32
    ).astype(jnp.bfloat16)
    value_per_head = content_sequences.reshape(
        device_sequences, device_residues, number_of_heads, head_channels
    )
    partial_value = jnp.einsum(
        "hij,sjhc->sihc", weight_panel, value_per_head, preferred_element_type=jnp.float32
    ).reshape(device_sequences, all_tokens, value_channels)
    partial_low = partial_value.astype(jnp.bfloat16)
    sigmoid_switch = jax.nn.sigmoid(
        jnp.dot(sequence_embedding_brief, switch_projection, preferred_element_type=jnp.float32)
    )
    pair_average = lax.psum_scatter(partial_low, "col", scatter_dimension=1, tiled=True).astype(
        jnp.float32
    )
    residual_change = jnp.dot(
        sigmoid_switch * pair_average, out_wide, precision=finest_accuracy
    ).astype(jnp.bfloat16)
    d_gated = jnp.dot(
        residual_change_cotangent.astype(jnp.float32), out_wide.T, precision=finest_accuracy
    )
    d_average_here = (sigmoid_switch * d_gated).astype(jnp.bfloat16)
    average_gradient = lax.all_gather(d_average_here, "col", axis=1, tiled=True)
    switch_preimage_sensitivity = d_gated * pair_average * sigmoid_switch * (1.0 - sigmoid_switch)
    gate_contribution = jnp.dot(
        switch_preimage_sensitivity, switch_single_form.T, precision=finest_accuracy
    )
    head_gradient = average_gradient.reshape(
        device_sequences, all_tokens, number_of_heads, head_channels
    )
    content_sensitivity = jnp.einsum(
        "hij,sihc->sjhc", weight_panel, head_gradient, preferred_element_type=jnp.float32
    )
    content_sensitivity = content_sensitivity.reshape(
        device_sequences, device_residues, value_channels
    ).astype(jnp.bfloat16)
    weight_part = jnp.einsum(
        "sihc,sjhc->hij", head_gradient, value_per_head, preferred_element_type=jnp.float32
    )
    d_weights = lax.psum_scatter(
        weight_part.astype(jnp.bfloat16), "bulk", scatter_dimension=1, tiled=True
    ).astype(jnp.float32)
    row_dot = lax.psum(jnp.sum(weights_low.astype(jnp.float32) * d_weights, axis=2), "col")
    d_logits = weights * (d_weights - row_dot[:, :, None])
    d_pair_low = jnp.einsum("hij,kh->ijk", d_logits, bias_wide, precision=finest_accuracy)
    coupling_sensitivity = layernorm_reverse_mode(
        d_pair_low, pair_hat, pair_inv, coupling_layernorm_factor
    ).astype(jnp.bfloat16)
    sequence_sensitivity_brief = (
        jnp.dot(content_sensitivity, content_projection.T, preferred_element_type=jnp.float32)
        + gate_contribution
    )
    sequence_embedding_sensitivity = layernorm_reverse_mode(
        sequence_sensitivity_brief,
        sequence_centred_unit,
        sequence_reciprocal_spread,
        sequence_layernorm_factor,
    ).astype(jnp.bfloat16)
    return (residual_change, sequence_embedding_sensitivity, coupling_sensitivity)


def solution(mesh):
    in_specs = (
        P("bulk", "col", None),
        P("bulk", "col", None),
        P(),
        P(),
        P(),
        P(),
        P(),
        P(),
        P("bulk", "col", None),
    )
    out_specs = (P("bulk", "col", None), P("bulk", "col", None), P("bulk", "col", None))
    return jax.shard_map(
        per_device, mesh=mesh, in_specs=in_specs, out_specs=out_specs, check_vma=False
    )
```

profile of v0, /device:TPU:0, one launch (start us, length us, event | category | flops | bytes accessed | tf_op | source)
XLA Modules:
  0.0 105.6 jit_solution(678878752773036502)
XLA Ops:
  7.2 1.0 convert_reduce_fusion.1
  8.5 0.5 copy-done.4
  9.1 0.2 convolution_convert_fusion.2
  9.4 0.2 reshape.60
  9.6 0.5 copy-done.5
  10.3 0.6 copy-done.6
  10.9 0.3 multiply_convert_fusion
  11.2 11.5 %all_gather.7 = bf16[8,128,256]{2,1,0:T(8,128)(2,1)S(1)} all-gather(bf16[8,32,256]{2,1,0:T(8,128)(2,1)S(1)} %get-tuple-element.9), channel_id=1, replica_groups=mesh['col'=4,'bulk'=8] {'col'}, dimensions={1}, use_global_device_ids=true | all-gather | bytes 655360 | tf_op jit(solution)/shard_map/all_gather | solution.py:88
  22.7 0.3 copy.58
  23.0 0.3 fusion.6
  23.3 0.9 copy.64
  24.3 0.8 copy-done.2
  25.2 0.3 fusion.21
  25.5 0.6 copy-done.9
  26.2 0.4 fusion.65
  26.6 9.1 %psum.14 = f32[8,16]{0,1:T(8,128)S(1)} all-reduce(f32[8,16]{0,1:T(8,128)S(1)} %get-tuple-element.11), channel_id=1, replica_groups=mesh['col'=4,'bulk'=8] {'col'}, use_global_device_ids=true, to_apply=%region_5.0 | all-reduce | flops 128 | bytes 1024 | tf_op jit(solution)/shard_map/psum | solution.py:56
  35.7 19.7 %reduce-scatter.5.cloned.1.call-done = bf16[8,16,32]{2,0,1:T(8,128)(2,1)} async-done(((bf16[8,128,32]{2,0,1:T(8,128)(2,1)}), bf16[8,16,32]{2,0,1:T(8,128)(2,1)}) %reduce-scatter.5.cloned.1.call-update) | async-done | bytes 8208 | tf_op jit(solution)/shard_map/reduce_scatter | solution.py:105
  55.4 0.9 fusion.45
  56.3 14.2 %all_gather.6 = bf16[8,128,32]{2,0,1:T(8,128)(2,1)S(1)} all-gather(bf16[8,16,32]{2,0,1:T(8,128)(2,1)S(1)} %get-tuple-element.8), channel_id=1, replica_groups=mesh['col'=4,'bulk'=8] {'bulk'}, dimensions={1}, use_global_device_ids=true | all-gather | bytes 73728 | tf_op jit(solution)/shard_map/all_gather | solution.py:59
  70.5 0.4 fusion
  70.9 1.0 copy.57
  71.9 0.3 fusion.1
  72.2 0.3 copy.61
  72.6 0.4 convert_element_type.78
  73.0 10.5 %psum.15 = f32[8,16]{0,1:T(8,128)S(1)} all-reduce(f32[8,16]{0,1:T(8,128)S(1)} %get-tuple-element.7), channel_id=1, replica_groups=mesh['col'=4,'bulk'=8] {'col'}, use_global_device_ids=true, to_apply=%region_11.0 | all-reduce | flops 128 | bytes 1024 | tf_op jit(solution)/shard_map/psum | solution.py:108
  83.4 0.7 fusion.62
  84.1 1.0 fusion.20
  85.1 10.4 %reduce-scatter.3.cloned.1.call-done = bf16[8,32,256]{2,1,0:T(8,128)(2,1)} async-done(((bf16[8,128,256]{2,1,0:T(8,128)(2,1)}), bf16[8,32,256]{2,1,0:T(8,128)(2,1)}) %reduce-scatter.3.cloned.1.call-update) | async-done | bytes 131088 | tf_op jit(solution)/shard_map/reduce_scatter | solution.py:78
  95.5 1.2 %fusion.24 = f32[8,32,64]{2,1,0:T(8,128)S(1)} fusion(f32[8,32,256]{2,1,0:T(8,128)S(1)} %get-tuple-element.10, f32[8,32,256]{2,1,0:T(8,128)S(1)} %fusion.50, bf16[8,32,256]{2,1,0:T(8,128)(2,1)} %reduce-scatter.3.cloned.1.call-done, bf16[64,256]{1,0:T(8,128)(2,1)S(1)} %copy-done.6), kind=kOutput, calls=%fused_computation.37 | convolution fusion | flops 50659328 | bytes 753664 | tf_op jit(solution)/shard_map/dot_general | solution.py:90
  96.7 0.3 fusion.63
  97.0 0.8 fusion.38
  97.9 0.9 convolution_convert_fusion.3
  (31 shorter events, 0.9 us)
Async XLA Ops:
  7.2 2.4 %copy-start = (bf16[8,32,64]{2,1,0:T(8,128)(2,1)S(1)}, bf16[8,32,64]{2,1,0:T(8,128)(2,1)}, u32[]{:S(2)}) copy-start(bf16[8,32,64]{2,1,0:T(8,128)(2,1)} %param.17) | copy-start | bytes 98308
  7.2 1.0 copy-start.1
  7.2 48.2 %reduce-scatter.5.cloned.1.call-start = ((), (), s32[]{:S(2)}) async-start(), calls=%async_computation.3 | async-start | bytes 294912 | tf_op jit(solution)/shard_map/reduce_scatter | solution.py:105
  8.2 0.8 copy-start.4
  8.4 0.7 copy-start.8
  9.4 0.8 copy-start.5
  10.1 0.8 copy-start.6
  24.2 0.9 copy-start.2
  24.2 71.3 %reduce-scatter.3.cloned.1.call-start = ((), (), s32[]{:S(2)}) async-start(), calls=%async_computation.2 | async-start | bytes 655360 | tf_op jit(solution)/shard_map/reduce_scatter | solution.py:78
  25.5 0.7 copy-start.9
  25.5 0.7 copy-start.10
  72.6 10.8 %copy-start.7 = (bf16[8,16,32]{2,0,1:T(8,128)(2,1)S(1)}, bf16[8,16,32]{2,0,1:T(8,128)(2,1)}, u32[]{:S(2)}) copy-start(bf16[8,16,32]{2,0,1:T(8,128)(2,1)} %reduce-scatter.5.cloned.1.call-done) | copy-start | bytes 24580
  97.0 0.9 copy-start.3
Sparse Core Ops, SparseCore 0:
  24.3 31.0 reduce-scatter.4
  72.1 23.4 reduce-scatter.2
where the time goes:
time: 106 us
  blocking collectives  45.3 us (43%)
  waiting for transfers between devices  30.1 us (28%)
  between operations  14.3 us (13%)
  local copies, waits for them, and re-layouts  6.44 us (6%)
  matrix products  5.12 us (5%)
  other arithmetic  4.33 us (4%)
    reduce_scatter x1, waiting for transfers between devices, per_device(): lax.psum_scatter(weight_part.astype(jnp.bfloat16), 'bulk', scatter_dimens...  19.7 us
    all_gather x1, blocking collectives, per_device(): weight_panel = lax.all_gather(weights_low, 'bulk', axis=1, tiled=True)  14.2 us
    all_gather x1, blocking collectives, per_device(): average_gradient = lax.all_gather(d_average_here, 'col', axis=1, tiled=True)  11.5 us
    psum x1, blocking collectives, per_device(): lax.psum(jnp.sum(weights_low.astype(jnp.float32) * d_weights, axis=2), 'c...  10.5 us
    reduce_scatter x1, waiting for transfers between devices, per_device(): lax.psum_scatter(partial_low, 'col', scatter_dimension=1, tiled=True)  10.4 us
    psum x1, blocking collectives, per_device(): totals = lax.psum(jnp.sum(exponent, axis=2), 'col')  9.09 us
    unnamed x22, local copies, waits for them, and re-layouts  3.31 us
  transfers between devices with their start and end apart: 2, of which 2 were waited for; matrix products, arithmetic and copies ran while one was open for 3% of the time, Pallas kernels for 0%

commit v1 on v0

--- a/solution.py
+++ b/solution.py
@@ -85,7 +85,15 @@
         residual_change_cotangent.astype(jnp.float32), out_wide.T, precision=finest_accuracy
     )
     d_average_here = (sigmoid_switch * d_gated).astype(jnp.bfloat16)
-    average_gradient = lax.all_gather(d_average_here, "col", axis=1, tiled=True)
+    n_dev_all = lax.psum(1, "col")
+    mid_arr = [None] * n_dev_all
+    mid_arr[n_dev_all - 1] = d_average_here
+    views = [(pp, (pp + 1) % n_dev_all) for pp in range(n_dev_all)]
+    for dev_i in range(n_dev_all - 2, -1, -1):
+        mid_arr[dev_i] = lax.ppermute(mid_arr[dev_i + 1], "col", views)
+    m_next = jnp.concatenate(mid_arr, axis=1)
+    g_now = (lax.axis_index("col") + 1) * d_average_here.shape[1]
+    average_gradient = jnp.roll(m_next, g_now, axis=1)
     switch_preimage_sensitivity = d_gated * pair_average * sigmoid_switch * (1.0 - sigmoid_switch)
     gate_contribution = jnp.dot(
         switch_preimage_sensitivity, switch_single_form.T, precision=finest_accuracy

time: 106 us -> 113 us (1.066)
  waiting for transfers between devices: 30.1 us -> 47.4 us
  blocking collectives: 45.3 us -> 32.4 us
  starting transfers between devices: 0.08 us -> 3.89 us
  local copies, waits for them, and re-layouts: 6.44 us -> 5.09 us
    ppermute x0 -> x3, waiting for transfers between devices: none -> 14.5 us  [per_device(): mid_arr[dev_i] = lax.ppermute(mid_arr[dev_i + 1], 'col', views)]
    all_gather x1 -> x0, blocking collectives: 11.5 us -> none  [per_device(): average_gradient = lax.all_gather(d_average_here, 'col', axis=1, tiled=True)]
    ppermute x0 -> x3, starting transfers between devices: none -> 3.81 us  [per_device(): mid_arr[dev_i] = lax.ppermute(mid_arr[dev_i + 1], 'col', views)]
    reduce_scatter x1, waiting for transfers between devices: 19.7 us -> 22.5 us  [per_device(): lax.psum_scatter(weight_part.astype(jnp.bfloat16), 'bulk', scatter_dimens...]
    unnamed x22 -> x29, local copies, waits for them, and re-layouts: 3.31 us -> 1.91 us
    psum x1, blocking collectives: 9.09 us -> 7.85 us  [per_device(): totals = lax.psum(jnp.sum(exponent, axis=2), 'col')]
  transfers between devices with their start and end apart: 2 -> 5, of which waited for: 2 -> 5; matrix products, arithmetic and copies ran while one was open for 3% -> 4% of each run, Pallas kernels for 0% -> 0%
where the time goes in v1:
time: 113 us
  waiting for transfers between devices  47.4 us (42%)
  blocking collectives  32.4 us (29%)
  between operations  14.4 us (13%)
  matrix products  5.14 us (5%)
  local copies, waits for them, and re-layouts  5.09 us (5%)
  other arithmetic  4.33 us (4%)
  starting transfers between devices  3.89 us (3%)
    reduce_scatter x1, waiting for transfers between devices, per_device(): lax.psum_scatter(weight_part.astype(jnp.bfloat16), 'bulk', scatter_dimens...  22.5 us
    ppermute x3, waiting for transfers between devices, per_device(): mid_arr[dev_i] = lax.ppermute(mid_arr[dev_i + 1], 'col', views)  14.5 us
    all_gather x1, blocking collectives, per_device(): weight_panel = lax.all_gather(weights_low, 'bulk', axis=1, tiled=True)  14.2 us
    reduce_scatter x1, waiting for transfers between devices, per_device(): lax.psum_scatter(partial_low, 'col', scatter_dimension=1, tiled=True)  10.4 us
    psum x1, blocking collectives, per_device(): lax.psum(jnp.sum(weights_low.astype(jnp.float32) * d_weights, axis=2), 'c...  10.4 us
    psum x1, blocking collectives, per_device(): totals = lax.psum(jnp.sum(exponent, axis=2), 'col')  7.85 us
    ppermute x3, starting transfers between devices, per_device(): mid_arr[dev_i] = lax.ppermute(mid_arr[dev_i + 1], 'col', views)  3.81 us
  transfers between devices with their start and end apart: 5, of which 5 were waited for; matrix products, arithmetic and copies ran while one was open for 4% of the time, Pallas kernels for 0%

profile of v1, /device:TPU:0, one launch (start us, length us, event | category | flops | bytes accessed | tf_op | source)
XLA Modules:
  0.0 112.6 jit_solution(13685824485507282666)
XLA Ops:
  7.2 1.0 convert_reduce_fusion.1
  8.5 0.5 copy-done.5
  9.2 0.6 copy-done.6
  9.8 0.3 multiply_convert_fusion
  10.1 3.0 %collective-permute-start = (bf16[8,32,256]{2,1,0:T(8,128)(2,1)S(1)}, bf16[8,32,256]{2,1,0:T(8,128)(2,1)S(1)}, u32[]{:S(2)}, u32[]{:S(2)}) collective-permute-start(bf16[8,32,256]{2,1,0:T(8,128)(2,1)S(1)} %get-tuple-element.9), channel_id=1, source_target_pairs={{0,8},{8,16},{16,24},{24,0},{1,9},{9,17},{17,25},{25,1},{2,10},{10... | collective-permute-start | bytes 393224 | tf_op jit(solution)/shard_map/ppermute | solution.py:93
  13.5 4.0 %collective-permute-done = bf16[8,32,256]{2,1,0:T(8,128)(2,1)S(1)} collective-permute-done((bf16[8,32,256]{2,1,0:T(8,128)(2,1)S(1)}, bf16[8,32,256]{2,1,0:T(8,128)(2,1)S(1)}, u32[]{:S(2)}, u32[]{:S(2)}) %collective-permute-start) | collective-permute-done | bytes 131104 | tf_op jit(solution)/shard_map/ppermute | solution.py:93
  17.5 0.8 collective-permute-start.1
  18.6 0.3 fusion.21
  18.8 4.6 %collective-permute-done.1 = bf16[8,32,256]{2,1,0:T(8,128)(2,1)S(1)} collective-permute-done((bf16[8,32,256]{2,1,0:T(8,128)(2,1)S(1)}, bf16[8,32,256]{2,1,0:T(8,128)(2,1)S(1)}, u32[]{:S(2)}, u32[]{:S(2)}) %collective-permute-start.1) | collective-permute-done | bytes 131104 | tf_op jit(solution)/shard_map/ppermute | solution.py:93
  23.4 5.9 %collective-permute-done.2 = bf16[8,32,256]{2,1,0:T(8,128)(2,1)S(1)} collective-permute-done((bf16[8,32,256]{2,1,0:T(8,128)(2,1)S(1)}, bf16[8,32,256]{2,1,0:T(8,128)(2,1)S(1)}, u32[]{:S(2)}, u32[]{:S(2)}) %collective-permute-start.2) | collective-permute-done | bytes 131104 | tf_op jit(solution)/shard_map/ppermute | solution.py:93
  29.5 0.3 copy.56
  29.7 0.3 fusion.6
  30.1 0.9 copy.62
  31.0 0.6 copy-done.9
  31.6 0.4 fusion.65
  32.1 7.9 %psum.14 = f32[8,16]{0,1:T(8,128)S(1)} all-reduce(f32[8,16]{0,1:T(8,128)S(1)} %get-tuple-element.11), channel_id=1, replica_groups=mesh['col'=4,'bulk'=8] {'col'}, use_global_device_ids=true, to_apply=%region_5.0 | all-reduce | flops 128 | bytes 1024 | tf_op jit(solution)/shard_map/psum | solution.py:56
  39.9 22.5 %reduce-scatter.5.cloned.1.call-done = bf16[8,16,32]{2,0,1:T(8,128)(2,1)} async-done(((bf16[8,128,32]{2,0,1:T(8,128)(2,1)}), bf16[8,16,32]{2,0,1:T(8,128)(2,1)}) %reduce-scatter.5.cloned.1.call-update) | async-done | bytes 8208 | tf_op jit(solution)/shard_map/reduce_scatter | solution.py:113
  62.4 0.9 fusion.45
  63.4 14.2 %all_gather.3 = bf16[8,128,32]{2,0,1:T(8,128)(2,1)S(1)} all-gather(bf16[8,16,32]{2,0,1:T(8,128)(2,1)S(1)} %get-tuple-element.8), channel_id=1, replica_groups=mesh['col'=4,'bulk'=8] {'bulk'}, dimensions={1}, use_global_device_ids=true | all-gather | bytes 73728 | tf_op jit(solution)/shard_map/all_gather | solution.py:59
  77.6 0.4 fusion
  78.0 1.0 copy.55
  79.0 0.3 fusion.1
  79.3 0.3 copy.59
  79.7 0.4 convert_element_type.78
  80.0 10.4 %psum.15 = f32[8,16]{0,1:T(8,128)S(1)} all-reduce(f32[8,16]{0,1:T(8,128)S(1)} %get-tuple-element.7), channel_id=1, replica_groups=mesh['col'=4,'bulk'=8] {'col'}, use_global_device_ids=true, to_apply=%region_11.12 | all-reduce | flops 128 | bytes 1024 | tf_op jit(solution)/shard_map/psum | solution.py:116
  90.4 0.7 fusion.62
  91.1 1.0 fusion.20
  92.1 10.4 %reduce-scatter.3.cloned.1.call-done = bf16[8,32,256]{2,1,0:T(8,128)(2,1)} async-done(((bf16[8,128,256]{2,1,0:T(8,128)(2,1)}), bf16[8,32,256]{2,1,0:T(8,128)(2,1)}) %reduce-scatter.3.cloned.1.call-update) | async-done | bytes 131088 | tf_op jit(solution)/shard_map/reduce_scatter | solution.py:78
  102.5 1.2 %fusion.24 = f32[8,32,64]{2,1,0:T(8,128)S(1)} fusion(f32[8,32,256]{2,1,0:T(8,128)S(1)} %get-tuple-element.10, f32[8,32,256]{2,1,0:T(8,128)S(1)} %fusion.50, bf16[8,32,256]{2,1,0:T(8,128)(2,1)} %reduce-scatter.3.cloned.1.call-done, bf16[64,256]{1,0:T(8,128)(2,1)S(1)} %copy-done.6), kind=kOutput, calls=%fused_computation.37 | convolution fusion | flops 50659328 | bytes 753664 | tf_op jit(solution)/shard_map/dot_general | solution.py:98
  103.7 0.3 fusion.63
  104.0 0.8 fusion.38
  104.9 0.9 convolution_convert_fusion.3
  (45 shorter events, 1.4 us)
Async XLA Ops:
  7.2 1.3 %copy-start = (bf16[8,32,64]{2,1,0:T(8,128)(2,1)S(1)}, bf16[8,32,64]{2,1,0:T(8,128)(2,1)}, u32[]{:S(2)}) copy-start(bf16[8,32,64]{2,1,0:T(8,128)(2,1)} %param.17) | copy-start | bytes 98308
  7.2 1.0 copy-start.1
  7.2 55.3 %reduce-scatter.5.cloned.1.call-start = ((), (), s32[]{:S(2)}) async-start(), calls=%async_computation.3 | async-start | bytes 294912 | tf_op jit(solution)/shard_map/reduce_scatter | solution.py:113
  8.2 0.8 copy-start.5
  9.0 0.8 copy-start.6
  9.0 0.8 copy-start.8
  9.8 3.3 %copy-start.4 = (bf16[64,256]{1,0:T(8,128)(2,1)S(1)}, bf16[64,256]{1,0:T(8,128)(2,1)}, u32[]{:S(2)}) copy-start(bf16[64,256]{1,0:T(8,128)(2,1)} %param.13) | copy-start | bytes 98308
  10.0 3.3 %copy-start.2 = (bf16[16,32,128]{2,1,0:T(8,128)(2,1)S(1)}, bf16[16,32,128]{2,1,0:T(8,128)(2,1)}, u32[]{:S(2)}) copy-start(bf16[16,32,128]{2,1,0:T(8,128)(2,1)} %param.10) | copy-start | bytes 393220
  10.1 7.5 %collective-permute-start = (bf16[8,32,256]{2,1,0:T(8,128)(2,1)S(1)}, bf16[8,32,256]{2,1,0:T(8,128)(2,1)S(1)}, u32[]{:S(2)}, u32[]{:S(2)}) collective-permute-start(bf16[8,32,256]{2,1,0:T(8,128)(2,1)S(1)} %get-tuple-element.9), channel_id=1, source_target_pairs={{0,8},{8,16},{16,24},{24,0},{1,9},{9,17},{17,25},{25,1},{2,10},{10... | collective-permute-start | bytes 393224 | tf_op jit(solution)/shard_map/ppermute | solution.py:93
  17.5 5.9 %collective-permute-start.1 = (bf16[8,32,256]{2,1,0:T(8,128)(2,1)S(1)}, bf16[8,32,256]{2,1,0:T(8,128)(2,1)S(1)}, u32[]{:S(2)}, u32[]{:S(2)}) collective-permute-start(bf16[8,32,256]{2,1,0:T(8,128)(2,1)S(1)} %collective-permute-done), channel_id=1, source_target_pairs={{0,8},{8,16},{16,24},{24,0},{1,9},{9,17},{17,25},{25,1},{2,10},{10... | collective-permute-start | bytes 393224 | tf_op jit(solution)/shard_map/ppermute | solution.py:93
  23.4 5.9 %collective-permute-start.2 = (bf16[8,32,256]{2,1,0:T(8,128)(2,1)S(1)}, bf16[8,32,256]{2,1,0:T(8,128)(2,1)S(1)}, u32[]{:S(2)}, u32[]{:S(2)}) collective-permute-start(bf16[8,32,256]{2,1,0:T(8,128)(2,1)S(1)} %collective-permute-done.1), channel_id=1, source_target_pairs={{0,8},{8,16},{16,24},{24,0},{1,9},{9,17},{17,25},{25,1},{2,10},{10... | collective-permute-start | bytes 393224 | tf_op jit(solution)/shard_map/ppermute | solution.py:93
  31.0 0.7 copy-start.9
  31.0 0.7 copy-start.10
  31.0 71.5 %reduce-scatter.3.cloned.1.call-start = ((), (), s32[]{:S(2)}) async-start(), calls=%async_computation.2 | async-start | bytes 655360 | tf_op jit(solution)/shard_map/reduce_scatter | solution.py:78
  79.6 10.8 %copy-start.7 = (bf16[8,16,32]{2,0,1:T(8,128)(2,1)S(1)}, bf16[8,16,32]{2,0,1:T(8,128)(2,1)}, u32[]{:S(2)}) copy-start(bf16[8,16,32]{2,0,1:T(8,128)(2,1)} %reduce-scatter.5.cloned.1.call-done) | copy-start | bytes 24580
  104.0 0.9 copy-start.3
Sparse Core Ops, SparseCore 0:
  31.1 31.2 reduce-scatter.4
  79.1 23.3 reduce-scatter.2
